TPU v7x, 128 devices: a whole 4x4x4 slice. The times are simulated.
128 devices in a mesh: doc: 8 (over x, core), term: 16 (over z, y).
Axes of the slice: x: 4, y: 4, z: 4, core: 2. Of those that a mesh axis runs over, the one named last changes fastest.
Arguments:
- query_states: bfloat16 [512, 32, 768], P('doc'), may hold values from -6 to 6
- token_ids: int32 [512, 32], P('doc'), may hold values from 0 to 30521, as said below
- transform_weight: bfloat16 [768, 768], replicated, may hold values from -0.21875 to 0.21875
- transform_bias: float32 [768], replicated, may hold values from -3 to 3
- norm_gain: float32 [768], replicated, may hold values from 0.5 to 1.5
- norm_bias: float32 [768], replicated, may hold values from -3 to 3
- decoder_weight: bfloat16 [768, 30720], P(None, 'term'), may hold values from -0.21875 to 0.21875
- decoder_bias: float32 [30720], P('term'), may hold values from -2.5 to 0.5
- candidates: int32 [512, 32], P('doc'), may hold values from 0 to 127, all different within a row; in each aligned block of 64 rows (0 to 63, 64 to 127, ...) at most 32 rows name the same one
- occupancy: int32 [128, 240], P('doc', 'term'), may hold values 0 or 1
- doc_blocks: bfloat16 [128, 240, 128, 128], P('doc', 'term'), may hold values from -0.046875 to 0.046875
Outputs:
- query_weights: bfloat16 [512, 30720], P('doc', 'term')
- scores: float32 [512, 32, 128], P('doc', None, 'term')
Inputs may be any that keep to these rules, and one draw needn't show every extreme that they name: `token_ids`: id 0 marks padding: a query has non-zero ids at its first positions, at least 8 of them, and 0 after them. `candidates`: A query names 32 different tiles; among the 64 queries of one doc index no tile is named by more than 32 of them.
All inputs are finite; a program needn't handle non-finite values. No bound on the sum of `occupancy` on one device may be relied on, other than what follows from the above.
Results may differ from a plain program's by a relative error of at most 0.0041.
Values may be sent and summed in bfloat16 or wider, within the bound.
A program may use at most 128 MiB of HBM per device.

v0:
```python
import jax
import jax.numpy as jnp
from jax import lax
from jax.sharding import PartitionSpec as P

VOCAB = 30522
MOST = 32


def tile_ranks(cand_rows, tile_total):
    tile_index = lax.iota(jnp.int32, tile_total)
    tile_hits = jnp.sum((cand_rows[..., None] == tile_index).astype(jnp.int32), axis=-2)
    tile_before = jnp.cumsum(tile_hits, axis=-2) - tile_hits
    return (tile_hits, tile_before)


def slot_sources(hits_by_tile, before_by_tile, capacity):
    row_total = hits_by_tile.shape[-1]
    slot_index = lax.iota(jnp.int32, capacity)
    chosen = (hits_by_tile[..., None, :] > 0) & (
        before_by_tile[..., None, :] == slot_index[:, None]
    )
    source_row = jnp.sum(jnp.where(chosen, lax.iota(jnp.int32, row_total), 0), axis=-1)
    return (source_row, jnp.any(chosen, axis=-1))


def body(
    query_states,
    token_ids,
    transform_weight,
    transform_bias,
    norm_gain,
    norm_bias,
    decoder_weight,
    decoder_bias,
    candidates,
    occupancy,
    doc_blocks,
):
    query_count, query_length, model_width = query_states.shape
    vocab_local = decoder_weight.shape[1]
    tile_local, blocks_local, tile_docs, block_terms = doc_blocks.shape
    cand_count = candidates.shape[1]
    term_index = lax.axis_index("term")
    doc_index = lax.axis_index("doc")
    doc_count = lax.axis_size("doc")
    term_count = lax.axis_size("term")
    tile_total = doc_count * tile_local
    hidden = (
        jnp.dot(
            query_states.reshape(query_count * query_length, model_width),
            transform_weight,
            preferred_element_type=jnp.float32,
        )
        + transform_bias
    )
    hidden = jax.nn.gelu(hidden, approximate=False)
    centred = hidden - jnp.mean(hidden, axis=-1, keepdims=True)
    spread = jnp.mean(centred * centred, axis=-1, keepdims=True)
    normed = (centred * lax.rsqrt(spread + 1e-06) * norm_gain + norm_bias).astype(jnp.bfloat16)
    logits = jnp.dot(normed, decoder_weight, preferred_element_type=jnp.float32) + decoder_bias
    activated = jnp.log1p(jnp.maximum(logits, 0.0)).reshape(query_count, query_length, vocab_local)
    live_mask = (token_ids != 0).astype(jnp.float32)[:, :, None]
    columns = term_index * vocab_local + lax.iota(jnp.int32, vocab_local)
    vocab_keep = (columns < VOCAB).astype(jnp.float32)
    weights = (jnp.max(activated * live_mask, axis=1) * vocab_keep).astype(jnp.bfloat16)
    own_hits, own_before = tile_ranks(candidates, tile_total)
    all_weights, all_cand = (
        lax.all_gather(weights, "doc", axis=0, tiled=True),
        lax.all_gather(candidates, "doc", axis=0, tiled=True),
    )
    local_cand = (all_cand - doc_index * tile_local).reshape(doc_count, query_count, cand_count)
    tile_hits, tile_before = tile_ranks(local_cand, tile_local)
    source_row, slot_valid = slot_sources(
        jnp.swapaxes(tile_hits, 1, 2), jnp.swapaxes(tile_before, 1, 2), MOST
    )
    flat_index = lax.iota(jnp.int32, doc_count)[:, None, None] * query_count + source_row
    buffer = jnp.take(all_weights, flat_index.reshape(-1), axis=0).reshape(
        doc_count, tile_local, MOST, vocab_local
    )
    buffer = buffer * slot_valid.astype(jnp.bfloat16)[..., None]
    occupied = occupancy.astype(jnp.bfloat16)
    masked = (
        buffer.reshape(doc_count, tile_local, MOST, blocks_local, block_terms)
        * occupied[None, :, None, :, None]
    )
    partial_value = jnp.einsum(
        "jtrbc,tbdc->jtrd", masked, doc_blocks, preferred_element_type=jnp.float32
    )
    slice_width = tile_docs // term_count
    score_total = lax.psum(partial_value, "term")
    score_share = lax.dynamic_slice_in_dim(score_total, term_index * slice_width, slice_width, 3)
    returned = lax.all_to_all(score_share, "doc", split_axis=0, concat_axis=1, tiled=True)
    slot_rank = jnp.take_along_axis(own_before, candidates, axis=1)
    flat_index = candidates * MOST + slot_rank
    scores = jnp.take(returned.reshape(-1, slice_width), flat_index.reshape(-1), axis=0)
    scores = scores.reshape(query_count, cand_count, slice_width)
    return (weights, scores)


def solution(mesh):
    placed = (
        P("doc", None, None),
        P("doc", None),
        P(),
        P(),
        P(),
        P(),
        P(None, "term"),
        P("term"),
        P("doc", None),
        P("doc", "term"),
        P("doc", "term", None, None),
    )
    return jax.shard_map(
        body,
        mesh=mesh,
        in_specs=placed,
        out_specs=(P("doc", "term"), P("doc", None, "term")),
        check_vma=False,
    )
```

profile of v0, /device:TPU:1, one launch (start us, length us, event | category | flops | bytes accessed | tf_op | source)
XLA Modules:
  0.0 286.4 jit_solution(9171432627118115750)
XLA Ops:
  7.2 0.9 copy.49
  8.2 0.9 copy-done
  9.1 17.5 %fusion.25 = (f32[2048]{0:T(1024)S(1)}, f32[2048,768]{0,1:T(8,128)S(1)}) fusion(f32[768]{0:T(1024)} %param.14, bf16[2048,768]{1,0:T(8,128)(2,1)S(1)} %bitcast.34, bf16[768,768]{1,0:T(8,128)(2,1)} %param.13), kind=kOutput, calls=%fused_computation.67 | convolution fusion | flops 2519726080 | bytes 10628096 | tf_op jit(solution)/shard_map/dot_general | solution.py:50
  26.6 0.7 multiply_reduce_fusion.1
  27.4 1.1 copy-done.4
  28.5 13.7 %multiply_reduce_fusion = f32[64,1920]{1,0:T(8,128)S(1)} fusion(f32[64,32]{1,0:T(8,128)S(1)} %compare_convert_fusion, f32[1920]{0:T(1024)S(1)} %copy-done.5, bf16[768,1920]{1,0:T(8,128)(2,1)S(1)} %copy-done.4, f32[2048,768]{0,1:T(8,128)S(1)} %get-tuple-element.7, f32[768]{0:T(1024)S(1)} %copy-done.6, f32[768]{0:T(1024)S(1)} %copy-done.7, ...), kind=kOutput, calls=%fused_computation.6 | convolution fusion | flops 6063267840 | bytes 9770496 | tf_op jit(solution)/shard_map/dot_general | solution.py:61
  42.2 0.7 multiply_convert_fusion
  43.0 14.4 %all-gather = s32[8,64,32]{1,2,0:T(8,128)S(1)} all-gather(s32[1,64,32]{1,2,0:T(8,128)S(1)} %bitcast.39), channel_id=1, replica_groups=mesh['doc'=8,'term'=16] {'doc'}, dimensions={0}, use_global_device_ids=true | all-gather | bytes 73728 | tf_op jit(solution)/shard_map/all_gather | solution.py:70
  57.4 0.3 convert_reduce_fusion
  57.9 6.6 %fusion.23 = s32[8,16,64]{1,0,2:T(8,128)S(1)} fusion(s32[8,64,16]{2,0,1:T(8,128)S(1)} %copy.56), kind=kOutput, calls=%fused_computation.43 | output fusion | flops 524288 | bytes 65536 | tf_op jit(solution)/shard_map/jit(cumsum)/reduce_window_sum | solution.py:13
  64.6 2.2 select_reduce_fusion
  67.1 2.3 fusion.17
  69.4 2.2 all-gather.3.cloned.1.call-done
  71.6 31.8 %gather_fusion = bf16[4096,1920]{1,0:T(8,128)(2,1)} fusion(bf16[512,1920]{1,0:T(8,128)(2,1)} %all-gather.3.cloned.1.call-done, s32[4096]{0:T(1024)S(1)} %broadcast_clamp_fusion), kind=kCustom, calls=%fused_computation | custom fusion | bytes 31473664 | tf_op jit(solution)/shard_map/jit(_take)/gather | solution.py:78
  103.4 27.2 %gather.18 = bf16[8,16,32,15,128]{4,3,2,1,0:T(8,128)(2,1)} reshape(bf16[4096,1920]{1,0:T(8,128)(2,1)} %gather_fusion) | data formatting | bytes 31457280 | tf_op jit(solution)/shard_map/jit(_take)/gather | solution.py:78
  130.6 14.0 %multiply_multiply_fusion = bf16[8,16,32,15,128]{4,3,2,1,0:T(8,128)(2,1)} fusion(bf16[8,16,32,15,128]{4,3,2,1,0:T(8,128)(2,1)} %gather.18, pred[8,16,32]{2,1,0:T(8,128)(4,1)S(1)} %get-tuple-element.4, bf16[16,15]{1,0:T(8,128)(2,1)S(1)} %convert_element_type.39, bf16[8,16,32]{2,1,0:T(8,128)(2,1)S(1)} %convert_element_type.38), kind=kLoop, calls=%fused_computation.3 | loop fusion | flops 23592960 | bytes 31470048 | tf_op jit(solution)/shard_map/mul | solution.py:84
  144.6 13.5 %fusion.18 = f32[8,16,32,128]{3,2,0,1:T(8,128)} fusion(bf16[16,15,128,128]{3,2,1,0:T(8,128)(2,1)} %param.21, bf16[8,16,32,15,128]{4,3,2,1,0:T(8,128)(2,1)} %multiply_multiply_fusion), kind=kOutput, calls=%fused_computation.39 | convolution fusion | flops 2013265920 | bytes 25690112 | tf_op jit(solution)/shard_map/jtrbc,tbdc->jtrd/dot_general | solution.py:87
  158.2 0.4 convert_reduce_fusion.1
  158.8 13.1 %gather_fusion.2 = s32[2048]{0:T(1024)S(1)} fusion(s32[64,128]{1,0:T(8,128)S(1)} %sub.26, s32[2048]{0:T(1024)S(1)} %reshape.174), kind=kCustom, calls=%fused_computation.2 | custom fusion | bytes 32768 | tf_op jit(solution)/shard_map/jit(take_along_axis)/gather | solution.py:94
  172.1 75.3 %all-reduce.2.cloned.1.call-done = f32[8,16,32,128]{3,2,0,1:T(8,128)} async-done(((f32[8,16,32,128]{3,2,0,1:T(8,128)}), f32[8,16,32,128]{3,2,0,1:T(8,128)}) %all-reduce.2.cloned.1.call-update) | async-done | bytes 2097168 | tf_op jit(solution)/shard_map/psum | solution.py:91
  247.4 2.2 constant_dynamic-slice_fusion
  249.6 0.6 copy.60
  250.2 0.9 reshape.192
  251.1 6.0 %all-to-all-start = ((f32[8,1,4096]{2,1,0:T(1,128)}), f32[8,1,4096]{2,1,0:T(1,128)S(1)}, u32[]{:S(2)}, u32[]{:S(2)}) async-start(f32[8,1,4096]{2,1,0:T(1,128)} %reshape.192), calls=%async_computation | async-start | bytes 262144 | tf_op jit(solution)/shard_map/all_to_all | solution.py:93
  257.1 5.3 %all-to-all-done = f32[8,1,4096]{2,1,0:T(1,128)S(1)} async-done(((f32[8,1,4096]{2,1,0:T(1,128)}), f32[8,1,4096]{2,1,0:T(1,128)S(1)}, u32[]{:S(2)}, u32[]{:S(2)}) %all-to-all-start) | async-done | bytes 131104 | tf_op jit(solution)/shard_map/all_to_all | solution.py:93
  262.4 0.5 broadcast.159
  262.9 1.0 reduce
  263.8 1.0 reshape.193
  264.8 3.2 %copy.66 = f32[8,16,32,8]{3,2,1,0:T(8,128)} copy(f32[8,16,32,8]{2,3,1,0:T(8,128)} %bitcast.38) | data formatting | bytes 262144 | tf_op jit(solution)/shard_map/reshape | solution.py:96
  268.0 9.1 %gather_fusion.1 = f32[2048,8]{1,0:T(8,128)} fusion(f32[4096,8]{1,0:T(8,128)} %bitcast.35, s32[2048]{0:T(1024)S(1)} %broadcast_clamp_fusion.1), kind=kCustom, calls=%fused_computation.1 | custom fusion | bytes 139264 | tf_op jit(solution)/shard_map/jit(_take)/gather | solution.py:96
  277.1 1.8 copy.63
  278.9 0.7 broadcast_select_fusion
  (44 shorter events, 1.3 us)
Async XLA Ops:
  7.2 1.9 copy-start
  7.2 64.4 %all-gather.3.cloned.1.call-start = ((), (), s32[]{:S(2)}) async-start(), calls=%async_computation.1 | async-start | bytes 2211840 | tf_op jit(solution)/shard_map/all_gather | solution.py:69
  26.6 1.8 copy-start.4
  26.6 1.8 copy-start.5
  26.6 1.8 copy-start.6
  26.6 1.8 copy-start.7
  28.4 14.5 %copy-start.3 = (s32[16,15]{1,0:T(8,128)S(1)}, s32[16,15]{1,0:T(8,128)}, u32[]{:S(2)}) copy-start(s32[16,15]{1,0:T(8,128)} %param.20) | copy-start | bytes 2884
  28.4 14.6 %copy-start.2 = (s32[64,32]{0,1:T(8,128)S(1)}, s32[64,32]{0,1:T(8,128)}, u32[]{:S(2)}) copy-start(s32[64,32]{0,1:T(8,128)} %param.19) | copy-start | bytes 24580
  42.9 204.5 %all-reduce.2.cloned.1.call-start = ((), (), s32[]{:S(2)}) async-start(), calls=%async_computation.2 | async-start | bytes 4194304 | tf_op jit(solution)/shard_map/psum | solution.py:91
  251.1 11.2 %all-to-all-start = ((f32[8,1,4096]{2,1,0:T(1,128)}), f32[8,1,4096]{2,1,0:T(1,128)S(1)}, u32[]{:S(2)}, u32[]{:S(2)}) async-start(f32[8,1,4096]{2,1,0:T(1,128)} %reshape.192), calls=%async_computation | async-start | bytes 262144 | tf_op jit(solution)/shard_map/all_to_all | solution.py:93
  264.8 14.8 %copy-start.1 = (bf16[64,32,768]{2,1,0:T(8,128)(2,1)S(1)}, bf16[64,32,768]{2,1,0:T(8,128)(2,1)}, u32[]{:S(2)}) copy-start(bf16[64,32,768]{2,1,0:T(8,128)(2,1)} %param.11) | copy-start | bytes 9437188
Sparse Core Ops, SparseCore 0:
  43.0 28.5 all-gather.2
  158.2 89.1 all-reduce.1
where the time goes:
time: 288 us; the launch traced here: 286 us
  local copies, waits for them, and re-layouts  95 us (33%)
  waiting for transfers between devices  82.8 us (29%)
  matrix products  44.7 us (16%)
  other arithmetic  29.1 us (10%)
  blocking collectives  14.4 us (5%)
  between operations  14.3 us (5%)
  starting transfers between devices  6.05 us (2%)
    psum x1, waiting for transfers between devices, body(): score_total = lax.psum(partial_value, 'term')  75.3 us
    gather x2, local copies, waits for them, and re-layouts, body(): jnp.take(all_weights, flat_index.reshape(-1), axis=0)  59 us
    dot_general x1, matrix products, body(): jnp.dot(query_states.reshape(query_count * query_length, model_width), tr...  17.5 us
    all_gather x1, blocking collectives, body(): lax.all_gather(candidates, 'doc', axis=0, tiled=True)  14.4 us
    mul x1, other arithmetic, body(): buffer.reshape(doc_count, tile_local, MOST, blocks_local, block_terms)  14 us
    dot_general x1, matrix products, body(): jnp.dot(normed, decoder_weight, preferred_element_type=jnp.float32)  13.7 us
    dot_general x1, matrix products, body(): jnp.einsum('jtrbc,tbdc->jtrd', masked, doc_blocks, preferred_element_type...  13.5 us
    gather x3, local copies, waits for them, and re-layouts, body(): slot_rank = jnp.take_along_axis(own_before, candidates, axis=1)  13.2 us
  transfers between devices with their start and end apart: 3, of which 3 were waited for; matrix products, arithmetic and copies ran while one was open for 9% of the time, Pallas kernels for 0%

commit v1 on v0

--- a/solution.py
+++ b/solution.py
@@ -1,3 +1,4 @@
+import functools
 import jax
 import jax.numpy as jnp
 from jax import lax
@@ -5,6 +6,13 @@
 
 VOCAB = 30522
 MOST = 32
+
+
+def watch_rails(mine_x, net_axis):
+    return jnp.sum(jax.lax.all_gather(mine_x, axis_name=net_axis), 0)
+
+
+take_frame = functools.partial(watch_rails, net_axis="term")
 
 
 def tile_ranks(cand_rows, tile_total):
@@ -88,7 +96,7 @@
         "jtrbc,tbdc->jtrd", masked, doc_blocks, preferred_element_type=jnp.float32
     )
     slice_width = tile_docs // term_count
-    score_total = lax.psum(partial_value, "term")
+    score_total = take_frame(partial_value)
     score_share = lax.dynamic_slice_in_dim(score_total, term_index * slice_width, slice_width, 3)
     returned = lax.all_to_all(score_share, "doc", split_axis=0, concat_axis=1, tiled=True)
     slot_rank = jnp.take_along_axis(own_before, candidates, axis=1)

time: 288 us -> 413 us (1.43)
  waiting for transfers between devices: 82.8 us -> 191 us
  other arithmetic: 29.1 us -> 42 us
    all_gather x0 -> x1, waiting for transfers between devices: none -> 183 us  [watch_rails(): return jnp.sum(jax.lax.all_gather(mine_x, axis_name=net_axis), 0)]
    psum x1 -> x0, waiting for transfers between devices: 75.3 us -> none  [body(): score_total = lax.psum(partial_value, 'term')]
    reduce_sum x0 -> x1, other arithmetic: none -> 12.9 us  [watch_rails(): return jnp.sum(jax.lax.all_gather(mine_x, axis_name=net_axis), 0)]
  transfers between devices with their start and end apart: 3 -> 3, of which waited for: 3 -> 3; matrix products, arithmetic and copies ran while one was open for 9% -> 6% of each run, Pallas kernels for 0% -> 0%
where the time goes in v1:
time: 413 us; the launch traced here: 412 us
  waiting for transfers between devices  191 us (46%)
  local copies, waits for them, and re-layouts  98 us (24%)
  matrix products  47.2 us (11%)
  other arithmetic  42 us (10%)
  blocking collectives  14.4 us (3%)
  between operations  14.3 us (3%)
  starting transfers between devices  5 us (1%)
    all_gather x1, waiting for transfers between devices, watch_rails(): return jnp.sum(jax.lax.all_gather(mine_x, axis_name=net_axis), 0)  183 us
    gather x2, local copies, waits for them, and re-layouts, body(): jnp.take(all_weights, flat_index.reshape(-1), axis=0)  59 us
    dot_general x1, matrix products, body(): jnp.dot(query_states.reshape(query_count * query_length, model_width), tr...  17.5 us
    dot_general x1, matrix products, body(): jnp.dot(normed, decoder_weight, preferred_element_type=jnp.float32)  16.3 us
    all_gather x1, blocking collectives, body(): lax.all_gather(candidates, 'doc', axis=0, tiled=True)  14.4 us
    mul x1, other arithmetic, body(): buffer.reshape(doc_count, tile_local, MOST, blocks_local, block_terms)  14 us
    dot_general x1, matrix products, body(): jnp.einsum('jtrbc,tbdc->jtrd', masked, doc_blocks, preferred_element_type...  13.5 us
    gather x3, local copies, waits for them, and re-layouts, body(): slot_rank = jnp.take_along_axis(own_before, candidates, axis=1)  13.2 us
  transfers between devices with their start and end apart: 3, of which 3 were waited for; matrix products, arithmetic and copies ran while one was open for 6% of the time, Pallas kernels for 0%

profile of v1, /device:TPU:1, one launch (start us, length us, event | category | flops | bytes accessed | tf_op | source)
XLA Modules:
  0.0 411.7 jit_solution(5122126522214062323)
XLA Ops:
  7.2 1.8 copy-done
  9.1 17.5 %fusion.25 = (f32[2048]{0:T(1024)S(1)}, f32[2048,768]{0,1:T(8,128)S(1)}) fusion(f32[768]{0:T(1024)} %param.14, bf16[2048,768]{1,0:T(8,128)(2,1)S(1)} %bitcast.35, bf16[768,768]{1,0:T(8,128)(2,1)} %param.13), kind=kOutput, calls=%fused_computation.67 | convolution fusion | flops 2519726080 | bytes 10628096 | tf_op jit(solution)/shard_map/dot_general | solution.py:58
  26.6 2.6 copy-done.2
  29.2 0.7 multiply_reduce_fusion.1
  30.1 16.3 %multiply_reduce_fusion = f32[64,1920]{1,0:T(8,128)S(1)} fusion(f32[64,32]{1,0:T(8,128)S(1)} %compare_convert_fusion, f32[1920]{0:T(1024)S(1)} %copy-done.6, bf16[768,1920]{1,0:T(8,128)(2,1)} %param.17, f32[2048,768]{0,1:T(8,128)} %copy-done.2, f32[768]{0:T(1024)S(1)} %copy-done.7, f32[768]{0:T(1024)S(1)} %copy-done.8, f32[2048]{0:T(1024)S(1)} %add_rsqrt_fusion, ...), kind=kOutput, calls=%fused_computation.6 | convolution fusion | flops 6063267840 | bytes 9770496 | tf_op jit(solution)/shard_map/dot_general | solution.py:69
  46.4 0.7 multiply_convert_fusion
  47.2 14.4 %all-gather.1 = s32[8,64,32]{1,2,0:T(8,128)S(1)} all-gather(s32[1,64,32]{1,2,0:T(8,128)S(1)} %bitcast.41), channel_id=1, replica_groups=mesh['doc'=8,'term'=16] {'doc'}, dimensions={0}, use_global_device_ids=true | all-gather | bytes 73728 | tf_op jit(solution)/shard_map/all_gather | solution.py:78
  61.7 0.3 convert_reduce_fusion
  62.1 6.6 %fusion.23 = s32[8,16,64]{1,0,2:T(8,128)S(1)} fusion(s32[8,64,16]{2,0,1:T(8,128)S(1)} %copy.53), kind=kOutput, calls=%fused_computation.43 | output fusion | flops 524288 | bytes 65536 | tf_op jit(solution)/shard_map/jit(cumsum)/reduce_window_sum | solution.py:21
  68.8 2.2 select_reduce_fusion
  71.3 2.3 fusion.17
  73.6 2.2 all-gather.5.cloned.1.call-done
  75.8 31.8 %gather_fusion = bf16[4096,1920]{1,0:T(8,128)(2,1)} fusion(bf16[512,1920]{1,0:T(8,128)(2,1)} %all-gather.5.cloned.1.call-done, s32[4096]{0:T(1024)S(1)} %broadcast_clamp_fusion), kind=kCustom, calls=%fused_computation | custom fusion | bytes 31473664 | tf_op jit(solution)/shard_map/jit(_take)/gather | solution.py:86
  107.7 27.2 %gather.18 = bf16[8,16,32,15,128]{4,3,2,1,0:T(8,128)(2,1)} reshape(bf16[4096,1920]{1,0:T(8,128)(2,1)} %gather_fusion) | data formatting | bytes 31457280 | tf_op jit(solution)/shard_map/jit(_take)/gather | solution.py:86
  134.8 14.0 %multiply_multiply_fusion = bf16[8,16,32,15,128]{4,3,2,1,0:T(8,128)(2,1)} fusion(bf16[8,16,32,15,128]{4,3,2,1,0:T(8,128)(2,1)} %gather.18, pred[8,16,32]{2,1,0:T(8,128)(4,1)S(1)} %get-tuple-element.4, bf16[16,15]{1,0:T(8,128)(2,1)S(1)} %convert_element_type.39, bf16[8,16,32]{2,1,0:T(8,128)(2,1)S(1)} %convert_element_type.38), kind=kLoop, calls=%fused_computation.3 | loop fusion | flops 23592960 | bytes 31470048 | tf_op jit(solution)/shard_map/mul | solution.py:92
  148.8 13.5 %fusion.18 = f32[8,16,32,128]{3,2,0,1:T(8,128)} fusion(bf16[16,15,128,128]{3,2,1,0:T(8,128)(2,1)} %param.21, bf16[8,16,32,15,128]{4,3,2,1,0:T(8,128)(2,1)} %multiply_multiply_fusion), kind=kOutput, calls=%fused_computation.39 | convolution fusion | flops 2013265920 | bytes 25690112 | tf_op jit(solution)/shard_map/jtrbc,tbdc->jtrd/dot_general | solution.py:95
  162.4 0.4 convert_reduce_fusion.1
  162.9 13.1 %gather_fusion.2 = s32[2048]{0:T(1024)S(1)} fusion(s32[64,128]{1,0:T(8,128)S(1)} %sub.26, s32[2048]{0:T(1024)S(1)} %reshape.174), kind=kCustom, calls=%fused_computation.2 | custom fusion | bytes 32768 | tf_op jit(solution)/shard_map/jit(take_along_axis)/gather | solution.py:102
  176.3 183.1 %all-gather.7.cloned.1.call-done = f32[128,16,32,128]{3,2,0,1:T(8,128)} async-done(((f32[8,16,32,128]{3,2,0,1:T(8,128)}), f32[128,16,32,128]{3,2,0,1:T(8,128)}) %all-gather.7.cloned.1.call-update) | async-done | bytes 33554448 | tf_op jit(solution)/shard_map/all_gather | solution.py:12
  359.5 12.9 %reduce_sum.59 = f32[8,16,32,128]{3,2,0,1:T(8,128)S(1)} reduce(f32[16,8,16,32,128]{4,3,1,0,2:T(8,128)} %bitcast.37, f32[]{:T(128)} %constant.31.clone.1), dimensions={0}, to_apply=%region_9.10 | reduce | flops 7864320 | bytes 35651588 | tf_op jit(solution)/shard_map/reduce_sum | solution.py:12
  372.4 2.0 constant_dynamic-slice_fusion
  374.4 2.2 copy.57
  376.5 0.9 reshape.193
  377.5 4.9 %all-to-all-start = ((f32[8,1,4096]{2,1,0:T(1,128)}), f32[8,1,4096]{2,1,0:T(1,128)S(1)}, u32[]{:S(2)}, u32[]{:S(2)}) async-start(f32[8,1,4096]{2,1,0:T(1,128)} %reshape.193), calls=%async_computation | async-start | bytes 262144 | tf_op jit(solution)/shard_map/all_to_all | solution.py:101
  382.4 5.3 %all-to-all-done = f32[8,1,4096]{2,1,0:T(1,128)S(1)} async-done(((f32[8,1,4096]{2,1,0:T(1,128)}), f32[8,1,4096]{2,1,0:T(1,128)S(1)}, u32[]{:S(2)}, u32[]{:S(2)}) %all-to-all-start) | async-done | bytes 131104 | tf_op jit(solution)/shard_map/all_to_all | solution.py:101
  387.7 0.5 broadcast.159
  388.2 1.0 reduce
  389.1 1.0 reshape.194
  390.1 3.2 copy.58
  393.3 9.1 %gather_fusion.1 = f32[2048,8]{1,0:T(8,128)} fusion(f32[4096,8]{1,0:T(8,128)} %bitcast.36, s32[2048]{0:T(1024)S(1)} %broadcast_clamp_fusion.1), kind=kCustom, calls=%fused_computation.1 | custom fusion | bytes 139264 | tf_op jit(solution)/shard_map/jit(_take)/gather | solution.py:104
  402.4 1.8 copy.59
  404.2 0.7 broadcast_select_fusion
  (47 shorter events, 1.4 us)
Async XLA Ops:
  7.2 1.9 copy-start
  7.2 68.7 %all-gather.5.cloned.1.call-start = ((), (), s32[]{:S(2)}) async-start(), calls=%async_computation.1 | async-start | bytes 2211840 | tf_op jit(solution)/shard_map/all_gather | solution.py:77
  26.6 2.7 copy-start.2
  26.6 3.4 copy-start.4
  26.6 3.5 copy-start.6
  26.6 3.5 copy-start.7
  26.6 3.5 copy-start.8
  30.1 17.1 %copy-start.3 = (s32[64,32]{0,1:T(8,128)S(1)}, s32[64,32]{0,1:T(8,128)}, u32[]{:S(2)}) copy-start(s32[64,32]{0,1:T(8,128)} %param.19) | copy-start | bytes 24580
  30.1 43.5 %copy-start.5 = (s32[16,15]{1,0:T(8,128)S(1)}, s32[16,15]{1,0:T(8,128)}, u32[]{:S(2)}) copy-start(s32[16,15]{1,0:T(8,128)} %param.20) | copy-start | bytes 2884
  47.1 312.3 %all-gather.7.cloned.1.call-start = ((), (), s32[]{:S(2)}) async-start(), calls=%async_computation.2 | async-start | bytes 35651584 | tf_op jit(solution)/shard_map/all_gather | solution.py:12
  377.5 10.2 %all-to-all-start = ((f32[8,1,4096]{2,1,0:T(1,128)}), f32[8,1,4096]{2,1,0:T(1,128)S(1)}, u32[]{:S(2)}, u32[]{:S(2)}) async-start(f32[8,1,4096]{2,1,0:T(1,128)} %reshape.193), calls=%async_computation | async-start | bytes 262144 | tf_op jit(solution)/shard_map/all_to_all | solution.py:101
  390.1 14.8 %copy-start.1 = (bf16[64,32,768]{2,1,0:T(8,128)(2,1)S(1)}, bf16[64,32,768]{2,1,0:T(8,128)(2,1)}, u32[]{:S(2)}) copy-start(bf16[64,32,768]{2,1,0:T(8,128)(2,1)} %param.11) | copy-start | bytes 9437188
Sparse Core Ops, SparseCore 0:
  47.3 28.5 all-gather.4
  162.4 197.0 all-gather.6
